TPU v7x, 512 devices: a whole 4x8x8 slice. The times are simulated.
512 devices in a mesh: dom: 128 (over z, y, core), rep: 4 (over x).
Axes of the slice: x: 4, y: 8, z: 8, core: 2. Of those that a mesh axis runs over, the one named last changes fastest.
Arguments:
- embedding: bfloat16 [131072, 128], P('dom'), may hold values from -6 to 6
- cotangent: bfloat16 [131072, 128], P('dom'), may hold values from -6 to 6
- degrees: int32 [131072], P('dom'), may hold values from 2 to 64
- tile_values: bfloat16 [128, 4, 32, 128, 128], P('dom', 'rep'), may hold values from 0 to 2, as said below
- tile_target: int32 [128, 4, 32], P('dom', 'rep'), may hold values from 0 to 7
- tile_source: int32 [128, 4, 32], P('dom', 'rep'), may hold values from 0 to 27
- live_tile_count: int32 [128, 4], P('dom', 'rep'), may hold values from 4 to 32, as said below
- send_rows: int32 [128, 128, 16], P('dom'), may hold values from 0 to 1023
- hub_rows: int32 [128, 4], P('dom'), may hold values from 0 to 1023
Outputs:
- layer_output: bfloat16 [131072, 128], P(('dom', 'rep'))
- embedding_gradient: bfloat16 [131072, 128], P(('dom', 'rep'))
Inputs may be any that keep to these rules, and one draw needn't show every extreme that they name: `tile_values`: each entry is an edge weight, zero where the two nodes share no edge. `live_tile_count`: slots at or past a device's count are not live; in every draw some device has all 32 slots live.
All inputs are finite; a program needn't handle non-finite values.
Results may differ from a plain program's by a relative error of at most 0.0048.
Values may be sent and summed in bfloat16 or wider, within the bound.
No kernel may reach another device: no remote copies, remote signals or barrier semaphores. Data moves between devices by JAX's collectives and lax.ppermute only.
A program may use at most 64 MiB of HBM per device.

v0:
```python
import jax
import jax.numpy as jnp
from jax import lax
from jax.sharding import PartitionSpec as P


def body(
    embedding,
    cotangent,
    degrees,
    tile_values,
    tile_target,
    tile_source,
    live_tile_count,
    send_rows,
    hub_rows,
):
    own_rows, feature_width = embedding.shape
    tile_size = tile_values.shape[-1]
    slot_grand_total = tile_values.shape[2]
    partitions = send_rows.shape[1]
    pair_rows = send_rows.shape[2]
    replicas = lax.axis_size("rep")
    replica_index = lax.axis_index("rep")
    root_inverse = lax.rsqrt(degrees.astype(jnp.float32))
    scaled = (root_inverse[:, None] * embedding.astype(jnp.float32)).astype(jnp.bfloat16)
    weighted = (root_inverse[:, None] * cotangent.astype(jnp.float32)).astype(jnp.bfloat16)
    arrived = lax.all_to_all(scaled[send_rows[0]], "dom", split_axis=0, concat_axis=0, tiled=True)
    hub_block = lax.all_gather(scaled[hub_rows[0]], "dom", axis=0, tiled=True)
    source = jnp.concatenate([scaled, arrived.reshape(-1, feature_width), hub_block], 0)
    source_blocks = source.shape[0] // tile_size
    source = source.reshape(source_blocks, tile_size, feature_width)
    target_blocks = own_rows // tile_size
    tile_matrix_block = tile_values[0, 0]
    targets = tile_target[0, 0]
    sources = tile_source[0, 0]
    tile_alive_mask = (
        jnp.arange(slot_grand_total, dtype=jnp.int32) < live_tile_count[0, 0]
    ).astype(jnp.float32)
    message_product = jnp.einsum(
        "ack,aky->acy", tile_matrix_block, source[sources], preferred_element_type=jnp.float32
    )
    target_onehot = (
        targets[None, :] == jnp.arange(target_blocks, dtype=jnp.int32)[:, None]
    ).astype(jnp.float32) * tile_alive_mask[None, :]
    forward = jnp.dot(
        target_onehot,
        message_product.reshape(slot_grand_total, -1),
        precision=lax.Precision.HIGHEST,
    )
    forward = forward.reshape(own_rows, feature_width)
    weighted_blocks = weighted.reshape(target_blocks, tile_size, feature_width)
    gathered_portion = jnp.einsum(
        "vzr,vzu->vru",
        tile_matrix_block,
        weighted_blocks[targets],
        preferred_element_type=jnp.float32,
    )
    source_onehot = (
        sources[None, :] == jnp.arange(source_blocks, dtype=jnp.int32)[:, None]
    ).astype(jnp.float32) * tile_alive_mask[None, :]
    slot_sums = jnp.dot(
        source_onehot,
        gathered_portion.reshape(slot_grand_total, -1),
        precision=lax.Precision.HIGHEST,
    )
    slot_sums = slot_sums.reshape(-1, feature_width)
    boundary_end = own_rows + partitions * pair_rows
    local_part = slot_sums[:own_rows]
    boundary_part = slot_sums[own_rows:boundary_end].reshape(partitions, pair_rows, feature_width)
    hub_part = slot_sums[boundary_end:]
    returned = lax.all_to_all(boundary_part, "dom", split_axis=0, concat_axis=0, tiled=True)
    gradient_part = local_part.at[send_rows[0]].add(returned)
    hub_total = lax.psum_scatter(hub_part, "dom", scatter_dimension=0, tiled=True)
    gradient_part = gradient_part.at[hub_rows[0]].add(hub_total)
    forward_sum, gradient_sum = (
        lax.psum_scatter(forward, "rep", scatter_dimension=0, tiled=True),
        lax.psum_scatter(gradient_part, "rep", scatter_dimension=0, tiled=True),
    )
    out_rows = own_rows // replicas
    my_root = lax.dynamic_slice_in_dim(root_inverse, replica_index * out_rows, out_rows, 0)
    layer_output = (my_root[:, None] * forward_sum).astype(jnp.bfloat16)
    embedding_gradient = (my_root[:, None] * gradient_sum).astype(jnp.bfloat16)
    return (layer_output, embedding_gradient)


def solution(mesh):
    placed = (
        P("dom", None),
        P("dom", None),
        P("dom"),
        P("dom", "rep", None, None, None),
        P("dom", "rep", None),
        P("dom", "rep", None),
        P("dom", "rep"),
        P("dom", None, None),
        P("dom", None),
    )
    return jax.shard_map(
        body,
        mesh=mesh,
        in_specs=placed,
        out_specs=(P(("dom", "rep"), None), P(("dom", "rep"), None)),
        check_vma=False,
    )
```

profile of v0, /device:TPU:8, one launch (start us, length us, event | category | flops | bytes accessed | tf_op | source)
XLA Modules:
  0.0 282.8 jit_solution(11773690477429332172)
XLA Ops:
  8.0 0.0 copy-start
  8.0 0.8 convert_rsqrt_fusion
  8.8 0.7 compare_select_fusion
  9.5 0.1 copy.16
  9.6 0.1 reshape.160
  9.7 1.2 multiply_convert_fusion
  10.9 0.0 copy-start.4
  10.9 8.0 %gather_fusion = bf16[2048,128]{1,0:T(8,128)(2,1)} fusion(bf16[1024,128]{1,0:T(8,128)(2,1)S(1)} %get-tuple-element.3, s32[2048]{0:T(1024)S(1)} %broadcast_clamp_fusion), kind=kCustom, calls=%fused_computation | custom fusion | bytes 1056768 | tf_op jit(solution)/shard_map/gather | solution.py:28
  19.0 17.8 %all-to-all-start = ((bf16[128,16,128]{2,1,0:T(8,128)(2,1)}), bf16[128,16,128]{2,1,0:T(8,128)(2,1)}, u32[]{:S(2)}, u32[]{:S(2)}) async-start(bf16[128,16,128]{2,1,0:T(8,128)(2,1)} %bitcast.3), calls=%async_computation | async-start | bytes 1048576 | tf_op jit(solution)/shard_map/all_to_all | solution.py:28
  36.8 0.0 all-reduce.3.cloned.1.call-start
  36.8 0.0 copy-done.4
  37.5 0.7 gather_fusion.3
  38.3 1.9 convolution_bitcast_fusion
  40.2 1.9 copy.20
  42.1 3.0 %fusion = f32[28,16384]{1,0:T(8,128)S(1)} fusion(f32[4,8,128,128]{3,2,1,0:T(8,128)S(1)} %bitcast.47, f32[32]{0:T(128)S(1)} %compare_convert_fusion, s32[32]{0:T(128)S(1)} %bitcast.53), kind=kOutput, calls=%fused_computation.6 | convolution fusion | flops 176162560 | bytes 3932416 | tf_op jit(solution)/shard_map/dot_general | solution.py:62
  45.1 0.0 copy-start.2
  45.1 1.3 copy-done.2
  46.5 0.0 slice-start
  46.5 0.9 slice.20
  47.4 0.0 all-reduce.3.cloned.1.call-update
  47.4 0.0 copy-start.5
  47.4 0.4 slice-done
  47.8 1.1 reshape.157
  48.9 0.6 gather_fusion.1
  49.5 50.6 %all-gather.1 = bf16[128,4,128]{2,1,0:T(4,128)(2,1)S(1)} all-gather(bf16[1,4,128]{2,1,0:T(4,128)(2,1)S(1)} %bitcast.52), channel_id=2, replica_groups=mesh['dom'=128,'rep'=4] {'dom'}, dimensions={0}, use_global_device_ids=true | all-gather | bytes 132096 | tf_op jit(solution)/shard_map/all_gather | solution.py:29
  100.2 0.0 all-to-all-done
  100.2 11.0 %all-to-all-start.1 = ((f32[128,16,128]{2,1,0:T(8,128)}), f32[128,16,128]{2,1,0:T(8,128)}, u32[]{:S(2)}, u32[]{:S(2)}) async-start(f32[128,16,128]{2,1,0:T(8,128)} %reshape.157), calls=%async_computation.2 | async-start | bytes 2097152 | tf_op jit(solution)/shard_map/all_to_all | solution.py:72
  111.2 0.2 reduce-scatter.3.cloned.1.call-start
  111.4 1.1 pad_maximum_fusion
  112.5 0.7 gather_fusion.2
  113.3 2.2 convolution_bitcast_fusion.1
  115.5 1.9 copy.18
  117.4 3.0 %fusion.3 = f32[8,16384]{1,0:T(8,128)} fusion(f32[4,8,128,128]{3,2,1,0:T(8,128)S(1)} %bitcast.48, f32[32]{0:T(128)S(1)} %compare_convert_fusion, s32[32]{0:T(128)S(1)} %bitcast.54), kind=kOutput, calls=%fused_computation.9 | convolution fusion | flops 50332160 | bytes 2621696 | tf_op jit(solution)/shard_map/dot_general | solution.py:46
  120.4 2.0 reshape.154
  122.4 0.0 reduce-scatter.3.cloned.1.call-update
  122.5 0.0 reduce-scatter.5.cloned.1.call-start
  122.5 0.1 slice.17
  122.6 1.3 dynamic-slice
  124.5 18.1 %all-to-all-done.1 = f32[128,16,128]{2,1,0:T(8,128)} async-done(((f32[128,16,128]{2,1,0:T(8,128)}), f32[128,16,128]{2,1,0:T(8,128)}, u32[]{:S(2)}, u32[]{:S(2)}) %all-to-all-start.1) | async-done | bytes 1048608 | tf_op jit(solution)/shard_map/all_to_all | solution.py:72
  142.6 12.0 %scatter_fusion = f32[1024,128]{1,0:T(8,128)S(1)} fusion(f32[1024,128]{1,0:T(8,128)S(1)} %slice.17, s32[2048]{0:T(1024)S(1)} %reshape.160, f32[2048,128]{1,0:T(8,128)} %bitcast.19), kind=kCustom, calls=%fused_computation.4 | custom fusion | flops 262144 | bytes 3153920 | tf_op jit(solution)/shard_map/scatter-add | solution.py:73
  154.7 92.1 %all-reduce.3.cloned.1.call-done = f32[512,128]{1,0:T(8,128)} async-done(((f32[512,128]{1,0:T(8,128)}), f32[512,128]{1,0:T(8,128)}) %all-reduce.3.cloned.1.call-update) | async-done | bytes 262160
  246.7 1.0 scatter_custom_fusion.1
  247.7 0.0 copy-start.1
  247.7 0.8 copy-done.1
  248.5 0.0 reduce-scatter.5.cloned.1.call-update
  248.6 0.1 dynamic_slice.3
  248.6 25.0 %reduce-scatter.5.cloned.1.call-done = f32[256,128]{1,0:T(8,128)} async-done(((f32[1024,128]{1,0:T(8,128)}), f32[256,128]{1,0:T(8,128)}) %reduce-scatter.5.cloned.1.call-update) | async-done | bytes 131088 | tf_op jit(solution)/shard_map/reduce_scatter | solution.py:78
  273.7 1.7 multiply_convert_fusion.2
  (16 shorter events, 0.1 us)
Async XLA Ops:
  8.0 30.3 %copy-start = (bf16[1,1,32,128,128]{4,3,2,1,0:T(8,128)(2,1)S(1)}, bf16[1,1,32,128,128]{4,3,2,1,0:T(8,128)(2,1)}, u32[]{:S(2)}) copy-start(bf16[1,1,32,128,128]{4,3,2,1,0:T(8,128)(2,1)} %param.12) | copy-start | bytes 3145732
  10.9 25.9 %copy-start.4 = (s32[1,1,32]{2,1,0:T(1,128)S(1)}, s32[1,1,32]{2,1,0:T(1,128)}, u32[]{:S(2)}) copy-start(s32[1,1,32]{2,1,0:T(1,128)} %param.13) | copy-start | bytes 388
  19.0 81.2 %all-to-all-start = ((bf16[128,16,128]{2,1,0:T(8,128)(2,1)}), bf16[128,16,128]{2,1,0:T(8,128)(2,1)}, u32[]{:S(2)}, u32[]{:S(2)}) async-start(bf16[128,16,128]{2,1,0:T(8,128)(2,1)} %bitcast.3), calls=%async_computation | async-start | bytes 1048576 | tf_op jit(solution)/shard_map/all_to_all | solution.py:28
  36.8 210.0 %all-reduce.3.cloned.1.call-start = ((), (), s32[]{:S(2)}) async-start(), calls=%async_computation.6 | async-start | bytes 524288
  40.2 1.9 copy-start.3
  45.1 1.3 copy-start.2
  46.5 1.3 slice-start
  47.4 1.5 copy-start.5
  100.2 42.5 %all-to-all-start.1 = ((f32[128,16,128]{2,1,0:T(8,128)}), f32[128,16,128]{2,1,0:T(8,128)}, u32[]{:S(2)}, u32[]{:S(2)}) async-start(f32[128,16,128]{2,1,0:T(8,128)} %reshape.157), calls=%async_computation.2 | async-start | bytes 2097152 | tf_op jit(solution)/shard_map/all_to_all | solution.py:72
  111.2 137.4 %reduce-scatter.3.cloned.1.call-start = ((), (), s32[]{:S(2)}) async-start(), calls=%async_computation.4 | async-start | bytes 655360 | tf_op jit(solution)/shard_map/reduce_scatter | solution.py:77
  120.4 2.1 slice-start.1
  122.5 151.2 %reduce-scatter.5.cloned.1.call-start = ((), (), s32[]{:S(2)}) async-start(), calls=%async_computation.5 | async-start | bytes 655360 | tf_op jit(solution)/shard_map/reduce_scatter | solution.py:78
  247.7 0.8 copy-start.1
Sparse Core Ops, SparseCore 0:
  47.5 199.1 all-reduce.2
Sparse Core Ops, SparseCore 1:
  122.5 27.8 reduce-scatter.2
  248.6 25.0 reduce-scatter.4
where the time goes:
time: 283 us
  waiting for transfers between devices  135 us (48%)
  blocking collectives  50.6 us (18%)
  starting transfers between devices  29.1 us (10%)
  local copies, waits for them, and re-layouts  22.1 us (8%)
  other arithmetic  18.6 us (7%)
  between operations  17 us (6%)
  matrix products  10.1 us (4%)
    unnamed x4, waiting for transfers between devices  92.1 us
    all_gather x1, blocking collectives, body(): hub_block = lax.all_gather(scaled[hub_rows[0]], 'dom', axis=0, tiled=True)  50.6 us
    reduce_scatter x1, waiting for transfers between devices, body(): lax.psum_scatter(gradient_part, 'rep', scatter_dimension=0, tiled=True)  25 us
    all_to_all x1, waiting for transfers between devices, body(): lax.all_to_all(boundary_part, 'dom', split_axis=0, concat_axis=0, tiled=T...  18.1 us
    all_to_all x1, starting transfers between devices, body(): lax.all_to_all(scaled[send_rows[0]], 'dom', split_axis=0, concat_axis=0,...  17.8 us
    scatter-add x1, other arithmetic, body(): gradient_part = local_part.at[send_rows[0]].add(returned)  12 us
    all_to_all x1, starting transfers between devices, body(): lax.all_to_all(boundary_part, 'dom', split_axis=0, concat_axis=0, tiled=T...  11 us
    gather x1, local copies, waits for them, and re-layouts, body(): scaled[send_rows[0]]  8.02 us
  transfers between devices with their start and end apart: 5, of which 3 were waited for; matrix products, arithmetic and copies ran while one was open for 13% of the time, Pallas kernels for 0%

commit v1 on v0

--- a/solution.py
+++ b/solution.py
@@ -26,7 +26,9 @@
     scaled = (root_inverse[:, None] * embedding.astype(jnp.float32)).astype(jnp.bfloat16)
     weighted = (root_inverse[:, None] * cotangent.astype(jnp.float32)).astype(jnp.bfloat16)
     arrived = lax.all_to_all(scaled[send_rows[0]], "dom", split_axis=0, concat_axis=0, tiled=True)
-    hub_block = lax.all_gather(scaled[hub_rows[0]], "dom", axis=0, tiled=True)
+    hub_block = jnp.concatenate(
+        lax.all_to_all(jnp.stack([scaled[hub_rows[0]]] * lax.axis_size("dom")), "dom", 0, 0), axis=0
+    )
     source = jnp.concatenate([scaled, arrived.reshape(-1, feature_width), hub_block], 0)
     source_blocks = source.shape[0] // tile_size
     source = source.reshape(source_blocks, tile_size, feature_width)

time: 283 us -> 305 us (1.078)
  waiting for transfers between devices: 135 us -> 199 us
  blocking collectives: 50.6 us -> 0 us
  starting transfers between devices: 29.1 us -> 36.1 us
    unnamed x4, waiting for transfers between devices: 92.1 us -> 146 us
    all_gather x1 -> x0, blocking collectives: 50.6 us -> none  [body(): hub_block = lax.all_gather(scaled[hub_rows[0]], 'dom', axis=0, tiled=True)]
    all_to_all x0 -> x1, starting transfers between devices: none -> 17.4 us  [body(): lax.all_to_all(jnp.stack([scaled[hub_rows[0]]] * lax.axis_size('dom')), '...]
    all_to_all x1, waiting for transfers between devices: 0.01 us -> 7.85 us  [body(): lax.all_to_all(scaled[send_rows[0]], 'dom', split_axis=0, concat_axis=0,...]
    all_to_all x1, starting transfers between devices: 17.8 us -> 11.9 us  [body(): lax.all_to_all(scaled[send_rows[0]], 'dom', split_axis=0, concat_axis=0,...]
    all_to_all x1, starting transfers between devices: 11 us -> 6.45 us  [body(): lax.all_to_all(boundary_part, 'dom', split_axis=0, concat_axis=0, tiled=T...]
  transfers between devices with their start and end apart: 5 -> 6, of which waited for: 3 -> 5; matrix products, arithmetic and copies ran while one was open for 13% -> 15% of each run, Pallas kernels for 0% -> 0%
where the time goes in v1:
time: 305 us
  waiting for transfers between devices  199 us (65%)
  starting transfers between devices  36.1 us (12%)
  local copies, waits for them, and re-layouts  22.8 us (7%)
  other arithmetic  19.3 us (6%)
  between operations  17 us (6%)
  matrix products  10.7 us (4%)
    unnamed x4, waiting for transfers between devices  146 us
    reduce_scatter x1, waiting for transfers between devices, body(): lax.psum_scatter(gradient_part, 'rep', scatter_dimension=0, tiled=True)  25 us
    all_to_all x1, waiting for transfers between devices, body(): lax.all_to_all(boundary_part, 'dom', split_axis=0, concat_axis=0, tiled=T...  17.9 us
    all_to_all x1, starting transfers between devices, body(): lax.all_to_all(jnp.stack([scaled[hub_rows[0]]] * lax.axis_size('dom')), '...  17.4 us
    scatter-add x1, other arithmetic, body(): gradient_part = local_part.at[send_rows[0]].add(returned)  12 us
    all_to_all x1, starting transfers between devices, body(): lax.all_to_all(scaled[send_rows[0]], 'dom', split_axis=0, concat_axis=0,...  11.9 us
    gather x1, local copies, waits for them, and re-layouts, body(): scaled[send_rows[0]]  7.98 us
    all_to_all x1, waiting for transfers between devices, body(): lax.all_to_all(scaled[send_rows[0]], 'dom', split_axis=0, concat_axis=0,...  7.85 us
  transfers between devices with their start and end apart: 6, of which 5 were waited for; matrix products, arithmetic and copies ran while one was open for 15% of the time, Pallas kernels for 0%

profile of v1, /device:TPU:8, one launch (start us, length us, event | category | flops | bytes accessed | tf_op | source)
XLA Modules:
  0.0 304.7 jit_solution(4639242432272159885)
XLA Ops:
  8.0 0.0 copy-start
  8.0 0.8 convert_rsqrt_fusion
  8.8 0.7 fusion.18
  9.5 1.2 multiply_convert_fusion
  10.7 0.6 gather_fusion.1
  11.3 0.7 stack.2
  12.0 17.4 %all-to-all-start.1 = ((bf16[128,4,128]{2,1,0:T(4,128)(2,1)}), bf16[128,4,128]{2,1,0:T(4,128)(2,1)S(1)}, u32[]{:S(2)}, u32[]{:S(2)}) async-start(bf16[128,4,128]{2,1,0:T(4,128)(2,1)} %stack.2), calls=%async_computation.1 | async-start | bytes 262144 | tf_op jit(solution)/shard_map/all_to_all | solution.py:30
  29.3 0.7 compare_select_fusion
  30.0 0.1 copy.16
  30.1 0.1 reshape.166
  30.2 0.0 copy-start.4
  30.2 8.0 %gather_fusion = bf16[2048,128]{1,0:T(8,128)(2,1)} fusion(bf16[1024,128]{1,0:T(8,128)(2,1)S(1)} %get-tuple-element.3, s32[2048]{0:T(1024)S(1)} %broadcast_clamp_fusion), kind=kCustom, calls=%fused_computation | custom fusion | bytes 1056768 | tf_op jit(solution)/shard_map/gather | solution.py:28
  38.2 0.7 gather_fusion.3
  39.0 2.3 all-to-all-done.1
  41.3 11.9 %all-to-all-start = ((bf16[128,16,128]{2,1,0:T(8,128)(2,1)}), bf16[128,16,128]{2,1,0:T(8,128)(2,1)}, u32[]{:S(2)}, u32[]{:S(2)}) async-start(bf16[128,16,128]{2,1,0:T(8,128)(2,1)} %bitcast.3), calls=%async_computation | async-start | bytes 1048576 | tf_op jit(solution)/shard_map/all_to_all | solution.py:28
  53.2 0.0 all-reduce.3.cloned.1.call-start
  53.3 1.8 convolution_bitcast_fusion
  55.1 1.9 copy.20
  57.7 3.7 %fusion = f32[28,16384]{1,0:T(8,128)S(1)} fusion(f32[4,8,128,128]{3,2,1,0:T(8,128)S(1)} %bitcast.46, f32[32]{0:T(128)S(1)} %compare_convert_fusion, s32[32]{0:T(128)} %bitcast.51), kind=kOutput, calls=%fused_computation.6 | convolution fusion | flops 176162560 | bytes 3932416 | tf_op jit(solution)/shard_map/dot_general | solution.py:64
  61.4 1.3 copy-done.2
  62.7 0.0 slice-start
  62.7 0.9 slice.20
  63.6 0.0 all-reduce.3.cloned.1.call-update
  63.7 0.0 copy-start.3
  63.7 0.4 slice-done
  64.1 1.1 reshape.163
  65.2 7.9 %all-to-all-done = bf16[128,16,128]{2,1,0:T(8,128)(2,1)} async-done(((bf16[128,16,128]{2,1,0:T(8,128)(2,1)}), bf16[128,16,128]{2,1,0:T(8,128)(2,1)}, u32[]{:S(2)}, u32[]{:S(2)}) %all-to-all-start) | async-done | bytes 524320 | tf_op jit(solution)/shard_map/all_to_all | solution.py:28
  73.0 6.4 %all-to-all-start.2 = ((f32[128,16,128]{2,1,0:T(8,128)}), f32[128,16,128]{2,1,0:T(8,128)}, u32[]{:S(2)}, u32[]{:S(2)}) async-start(f32[128,16,128]{2,1,0:T(8,128)} %reshape.163), calls=%async_computation.3 | async-start | bytes 2097152 | tf_op jit(solution)/shard_map/all_to_all | solution.py:74
  79.5 0.2 reduce-scatter.3.cloned.1.call-start
  79.7 1.1 pad_maximum_fusion
  80.8 0.7 gather_fusion.2
  81.6 2.2 convolution_bitcast_fusion.1
  83.8 1.9 copy.18
  85.7 3.0 fusion.3
  88.8 2.0 reshape.160
  90.8 0.0 reduce-scatter.3.cloned.1.call-update
  90.8 0.0 reduce-scatter.5.cloned.1.call-start
  90.9 0.1 slice.17
  91.0 1.3 dynamic-slice
  92.9 17.9 %all-to-all-done.2 = f32[128,16,128]{2,1,0:T(8,128)} async-done(((f32[128,16,128]{2,1,0:T(8,128)}), f32[128,16,128]{2,1,0:T(8,128)}, u32[]{:S(2)}, u32[]{:S(2)}) %all-to-all-start.2) | async-done | bytes 1048608 | tf_op jit(solution)/shard_map/all_to_all | solution.py:74
  110.8 12.0 %scatter_fusion = f32[1024,128]{1,0:T(8,128)S(1)} fusion(f32[1024,128]{1,0:T(8,128)S(1)} %slice.17, s32[2048]{0:T(1024)S(1)} %reshape.166, f32[2048,128]{1,0:T(8,128)} %bitcast.18), kind=kCustom, calls=%fused_computation.4 | custom fusion | flops 262144 | bytes 3153920 | tf_op jit(solution)/shard_map/scatter-add | solution.py:75
  122.9 145.8 %all-reduce.3.cloned.1.call-done = f32[512,128]{1,0:T(8,128)} async-done(((f32[512,128]{1,0:T(8,128)}), f32[512,128]{1,0:T(8,128)}) %all-reduce.3.cloned.1.call-update) | async-done | bytes 262160
  268.7 1.0 scatter_custom_fusion.1
  269.7 0.8 copy-done.1
  270.5 0.0 reduce-scatter.5.cloned.1.call-update
  270.5 0.1 dynamic_slice.3
  270.6 25.0 %reduce-scatter.5.cloned.1.call-done = f32[256,128]{1,0:T(8,128)} async-done(((f32[1024,128]{1,0:T(8,128)}), f32[256,128]{1,0:T(8,128)}) %reduce-scatter.5.cloned.1.call-update) | async-done | bytes 131088 | tf_op jit(solution)/shard_map/reduce_scatter | solution.py:80
  295.6 1.7 multiply_convert_fusion.2
  (20 shorter events, 0.1 us)
Async XLA Ops:
  8.0 45.3 %copy-start = (bf16[1,1,32,128,128]{4,3,2,1,0:T(8,128)(2,1)S(1)}, bf16[1,1,32,128,128]{4,3,2,1,0:T(8,128)(2,1)}, u32[]{:S(2)}) copy-start(bf16[1,1,32,128,128]{4,3,2,1,0:T(8,128)(2,1)} %param.12) | copy-start | bytes 3145732
  9.5 1.3 copy-start.6
  12.0 29.3 %all-to-all-start.1 = ((bf16[128,4,128]{2,1,0:T(4,128)(2,1)}), bf16[128,4,128]{2,1,0:T(4,128)(2,1)S(1)}, u32[]{:S(2)}, u32[]{:S(2)}) async-start(bf16[128,4,128]{2,1,0:T(4,128)(2,1)} %stack.2), calls=%async_computation.1 | async-start | bytes 262144 | tf_op jit(solution)/shard_map/all_to_all | solution.py:30
  30.2 8.0 %copy-start.4 = (s32[1,1,32]{2,1,0:T(1,128)S(1)}, s32[1,1,32]{2,1,0:T(1,128)}, u32[]{:S(2)}) copy-start(s32[1,1,32]{2,1,0:T(1,128)} %param.13) | copy-start | bytes 388
  41.3 31.8 %all-to-all-start = ((bf16[128,16,128]{2,1,0:T(8,128)(2,1)}), bf16[128,16,128]{2,1,0:T(8,128)(2,1)}, u32[]{:S(2)}, u32[]{:S(2)}) async-start(bf16[128,16,128]{2,1,0:T(8,128)(2,1)} %bitcast.3), calls=%async_computation | async-start | bytes 1048576 | tf_op jit(solution)/shard_map/all_to_all | solution.py:28
  53.2 215.5 %all-reduce.3.cloned.1.call-start = ((), (), s32[]{:S(2)}) async-start(), calls=%async_computation.7 | async-start | bytes 524288
  61.4 1.3 copy-start.2
  62.7 1.3 slice-start
  63.7 1.5 copy-start.3
  73.0 37.8 %all-to-all-start.2 = ((f32[128,16,128]{2,1,0:T(8,128)}), f32[128,16,128]{2,1,0:T(8,128)}, u32[]{:S(2)}, u32[]{:S(2)}) async-start(f32[128,16,128]{2,1,0:T(8,128)} %reshape.163), calls=%async_computation.3 | async-start | bytes 2097152 | tf_op jit(solution)/shard_map/all_to_all | solution.py:74
  79.5 191.1 %reduce-scatter.3.cloned.1.call-start = ((), (), s32[]{:S(2)}) async-start(), calls=%async_computation.5 | async-start | bytes 655360 | tf_op jit(solution)/shard_map/reduce_scatter | solution.py:79
  83.8 1.9 copy-start.5
  88.8 2.1 slice-start.1
  90.8 204.8 %reduce-scatter.5.cloned.1.call-start = ((), (), s32[]{:S(2)}) async-start(), calls=%async_computation.6 | async-start | bytes 655360 | tf_op jit(solution)/shard_map/reduce_scatter | solution.py:80
  269.7 0.8 copy-start.1
Sparse Core Ops, SparseCore 0:
  63.8 204.8 all-reduce.2
Sparse Core Ops, SparseCore 1:
  90.9 27.8 reduce-scatter.2
  270.6 25.0 reduce-scatter.4
